TPU v7x, 32 devices: a whole 2x2x4 slice. The times are simulated.
32 devices in a mesh: grp: 2 (over y), comp: 4 (over z), space: 4 (over x, core).
Axes of the slice: x: 2, y: 2, z: 4, core: 2. Of those that a mesh axis runs over, the one named last changes fastest.
Arguments:
- spectrum: float32 [2304, 4096], P('comp', ('grp', 'space')), parts along dimension 1, may hold values from -6 to 6
- wave_speed: float32 [36], replicated, may hold values from 0.25 to 2
- current_east: float32 [4096], P(('grp', 'space')), parts along dimension 0, may hold values from -3 to 3
- current_north: float32 [4096], P(('grp', 'space')), parts along dimension 0, may hold values from -3 to 3
- substeps: int32 [2304], replicated, may hold values from 1 to 4, as said below
- neighbours: int32 [4, 4096], P(None, ('grp', 'space')), parts along dimension 1, may hold values from 0 to 767, as said below
- blocks: bfloat16 [64, 64, 64], replicated, may hold values from -0.75 to 0.75
- quad_index: int32 [4, 64], replicated, may hold values from 0 to 35
- strength: float32 [64], replicated, may hold values from -1 to 1
Outputs:
- spectrum_out: float32 [2304, 4096], P('comp', ('grp', 'space')), parts along dimension 1
There are 2 independent parts, one for each index of `grp`. A program takes and returns all parts, laid end to end along the dimension named above; an argument that names none is the same for every part. Nothing has to cross between parts.
Inputs may be any that keep to these rules, and one draw needn't show every extreme that they name: `substeps`: component 0 takes 4. `neighbours`: the entry of row r for the slab's point q (counted within its slab) is q + 128 + o, with -128 <= o <= -1 for rows 0 and 2 and 1 <= o <= 128 for rows 1 and 3.
All inputs are finite; a program needn't handle non-finite values.
Results may differ from a plain program's by a relative error of at most 0.00031.
Values sent between devices are 32-bit elements; how exact they have to be, the bound alone decides.
A program may use at most 64 MiB of HBM per device.

v0:
```python
import functools
import math

import jax
import jax.numpy as jnp
import numpy as np
from jax import lax
from jax.experimental import pallas as pl
from jax.experimental.pallas import tpu as pltpu
from jax.sharding import PartitionSpec as P

NF = 36
ND = 64
SUB = 4
HALO = 128

courant_scale = 0.4
courant_limit = 0.45
source_step = 0.1

MESH = pl.DeviceIdType.MESH


def chunk_rows(rows):
    for size in (32, 24, 16, 8):
        if rows % size == 0:
            return size
    return rows


def sync(peers, spaces):
    me = lax.axis_index("comp")
    here = lax.axis_index("space")
    barrier = pltpu.get_barrier_semaphore()
    count = 0
    for k in range(1, peers):
        pl.semaphore_signal(
            barrier, inc=1, device_id={"comp": lax.rem(me + k, peers)}, device_id_type=MESH
        )
        count += 1
    if spaces:
        for k in (1, spaces - 1):
            pl.semaphore_signal(
                barrier, inc=1, device_id={"space": lax.rem(here + k, spaces)}, device_id_type=MESH
            )
            count += 1
    pl.semaphore_wait(barrier, count)


GATHER = lax.GatherDimensionNumbers(
    offset_dims=(),
    collapsed_slice_dims=(1,),
    start_index_map=(1,),
    operand_batching_dims=(0,),
    start_indices_batching_dims=(0,),
)


def take_lanes(values, index):
    return lax.gather(
        values,
        index[:, :, None],
        GATHER,
        slice_sizes=(1, 1),
        mode=lax.GatherScatterMode.PROMISE_IN_BOUNDS,
    )


def propagate_kernel(
    peers,
    spaces,
    chunk,
    block,
    field_ref,
    wave_ref,
    substeps_ref,
    trig_ref,
    east_ref,
    north_ref,
    neighbour_ref,
    points_ref,
    extended,
    finals,
    side_table,
    side_current,
    codes,
    currents,
    load_sem,
    side_send,
    side_recv,
    halo_send,
    halo_recv,
    piece_send,
    piece_recv,
    own_sem,
    turn_sem,
):
    me = lax.axis_index("comp")
    here = lax.axis_index("space")
    rows, width = field_ref.shape
    tiles = width // HALO
    reach = SUB * HALO
    chunks = rows // chunk
    has_left = here > 0
    has_right = here < spaces - 1
    odd = lax.rem(here, 2)
    goes_first = odd == jnp.where(here < spaces // 2, 0, 1)

    load = pltpu.make_async_copy(field_ref, extended.at[:, pl.ds(reach, width)], load_sem)
    load.start()

    sync(peers, spaces)

    left = {"space": jnp.maximum(here - 1, 0)}
    right = {"space": jnp.minimum(here + 1, spaces - 1)}

    def remote(source, target, send, recv, device):
        return pltpu.make_async_remote_copy(
            src_ref=source,
            dst_ref=target,
            send_sem=send,
            recv_sem=recv,
            device_id=device,
            device_id_type=MESH,
        )

    def sides():
        copies = []
        for side, start, device in ((1, 0, left), (0, width - reach, right)):
            part = pl.ds(start, reach)
            pairs = (
                (neighbour_ref.at[:, part], side_table.at[side]),
                (east_ref.at[:, part], side_current.at[side, 0]),
                (north_ref.at[:, part], side_current.at[side, 1]),
            )
            copies.append(
                [
                    remote(source, target, side_send.at[side, i], side_recv.at[side, i], device)
                    for i, (source, target) in enumerate(pairs)
                ]
            )
        return copies

    def halo(first, count, sem):
        part = pl.ds(first, count)
        to_left = remote(
            field_ref.at[part, pl.ds(0, reach)],
            extended.at[part, pl.ds(reach + width, reach)],
            halo_send.at[1],
            halo_recv.at[1, sem],
            left,
        )
        to_right = remote(
            field_ref.at[part, pl.ds(width - reach, reach)],
            extended.at[part, pl.ds(0, reach)],
            halo_send.at[0],
            halo_recv.at[0, sem],
            right,
        )
        return to_left, to_right

    def rows_of(c):
        return pl.multiple_of(c * chunk, 8)

    to_left_sides, to_right_sides = sides()

    @pl.when(has_left)
    def _():
        for copy in to_left_sides:
            copy.start()

    @pl.when(has_right)
    def _():
        for copy in to_right_sides:
            copy.start()

    def start_halo(c, carry):
        to_left, to_right = halo(rows_of(c), chunk, c)

        @pl.when(has_left)
        def _():
            to_left.start()

        @pl.when(has_right)
        def _():
            to_right.start()

        return carry

    lax.fori_loop(0, chunks, start_halo, 0)

    lane = lax.broadcasted_iota(jnp.int32, (4, HALO), 1)
    for side, missing in ((0, jnp.logical_not(has_left)), (1, jnp.logical_not(has_right))):

        @pl.when(missing)
        def _(side=side):
            first = (tiles - SUB) * HALO if side == 0 else 0
            for i in range(SUB):
                part = pl.ds(i * HALO, HALO)
                side_table[side, :, part] = lane + (first + (i + 1) * HALO)
            side_current[side] = jnp.zeros((2, 1, reach), jnp.float32)
            start = 0 if side == 0 else reach + width

            def clear(g, carry):
                at = pl.ds(pl.multiple_of(g * 8, 8), 8)
                extended[at, pl.ds(start, reach)] = jnp.zeros((8, reach), jnp.float32)
                return carry

            lax.fori_loop(0, rows // 8, clear, 0)

    def spread(row):
        return jnp.broadcast_to(row, (8, HALO))

    def fill(e, table_ref, east_row, north_row, tile, place):
        for d in range(4):
            codes[d, e] = spread(table_ref[d : d + 1, place] - tile * HALO)
        currents[0, e] = spread(east_row[:, place])
        currents[1, e] = spread(north_row[:, place])

    def fill_own(j, carry):
        fill(j + SUB, neighbour_ref, east_ref, north_ref, j, pl.ds(pl.multiple_of(j * HALO, HALO), HALO))
        return carry

    lax.fori_loop(0, tiles, fill_own, 0)

    @pl.when(has_right)
    def _():
        for copy in to_left_sides:
            copy.wait_recv()

    @pl.when(has_left)
    def _():
        for copy in to_right_sides:
            copy.wait_recv()

    for i in range(SUB):
        place = pl.ds(i * HALO, HALO)
        fill(i, side_table.at[0], side_current.at[0, 0], side_current.at[0, 1], tiles - SUB + i, place)
        fill(
            SUB + tiles + i, side_table.at[1], side_current.at[1, 0], side_current.at[1, 1], i, place
        )

    sublane = lax.broadcasted_iota(jnp.int32, (8, HALO), 0)
    window = block + 2 * SUB

    def upwind(before, own, after, code, index):
        picked = jnp.where(code >= 2 * HALO, take_lanes(after, index), take_lanes(own, index))
        return jnp.where(code < HALO, take_lanes(before, index), picked)

    def strip(row, b):
        at = pl.ds(row, 8)
        component = me * rows + row
        speed = wave_ref[component // ND]
        turn = pl.ds(pl.multiple_of(lax.rem(component, ND), 8), 8)
        own_x = trig_ref[0, turn, :] * speed
        own_y = trig_ref[1, turn, :] * speed
        taken = jnp.full((8, HALO), substeps_ref[component], jnp.int32)
        for i in range(1, 8):
            taken = jnp.where(sublane == i, substeps_ref[component + i], taken)
        scale = courant_scale / taken.astype(jnp.float32)
        base = b * block
        values = [
            extended[at, pl.ds(pl.multiple_of((base + i) * HALO, HALO), HALO)] for i in range(window)
        ]
        along = {}
        for i in range(1, window - 1):
            entry = []
            for axis, own in ((0, own_x), (1, own_y)):
                moved = (own + currents[axis, base + i]) * scale
                moved = jnp.clip(moved, -courant_limit, courant_limit)
                code = jnp.where(moved > 0.0, codes[2 * axis, base + i], codes[2 * axis + 1, base + i])
                entry.append((jnp.abs(moved), code, jnp.bitwise_and(code, HALO - 1)))
            along[i] = entry
        for s in range(SUB):
            latest = list(values)
            for i in range(s + 1, window - 1 - s):
                own = values[i]
                change = None
                for size, code, index in along[i]:
                    term = size * (own - upwind(values[i - 1], own, values[i + 1], code, index))
                    change = term if change is None else change + term
                if s > 0:
                    change = jnp.where(taken > s, change, 0.0)
                latest[i] = own - change
            values = latest
        for i in range(block):
            finals[base + i, at] = values[SUB + i]

    def piece(k, first, count):
        target = lax.rem(me + k, peers)
        return remote(
            finals.at[target, pl.ds(first, count)],
            points_ref.at[pl.ds(pl.multiple_of(me * rows + first, 8), count)],
            piece_send.at[k],
            piece_recv.at[k],
            {"comp": target},
        )

    order = sorted(range(1, peers), key=lambda k: abs(k - peers / 2))
    load.wait()

    def step(c, carry):
        first = rows_of(c)
        to_left, to_right = halo(first, chunk, c)

        @pl.when(has_right)
        def _():
            to_left.wait_recv()

        @pl.when(has_left)
        def _():
            to_right.wait_recv()

        def per_strip(g, inner):
            row = pl.multiple_of(first + g * 8, 8)

            def per_block(b, deepest):
                strip(row, b)
                return deepest

            if tiles == block:
                strip(row, 0)
                return inner
            return lax.fori_loop(0, tiles // block, per_block, inner)

        lax.fori_loop(0, chunk // 8, per_strip, 0)

        @pl.when(goes_first)
        def _():
            for k in order:
                piece(k, first, chunk).start()

        return carry

    lax.fori_loop(0, chunks, step, 0)
    own = pltpu.make_async_copy(
        finals.at[me], points_ref.at[pl.ds(pl.multiple_of(me * rows, 8), rows)], own_sem
    )
    own.start()

    @pl.when(jnp.logical_not(goes_first))
    def _():
        pl.semaphore_wait(turn_sem, 1)
        for k in order:
            piece(k, 0, rows).start()

    for k in order:
        piece(k, 0, rows).wait_send()

    @pl.when(goes_first)
    def _():
        partner = here + 1 - 2 * odd
        pl.semaphore_signal(turn_sem, inc=1, device_id={"space": partner}, device_id_type=MESH)

    own.wait()
    to_left, to_right = halo(0, rows, 0)

    @pl.when(has_left)
    def _():
        to_left.wait_send()
        for copy in to_left_sides:
            copy.wait_send()

    @pl.when(has_right)
    def _():
        to_right.wait_send()
        for copy in to_right_sides:
            copy.wait_send()

    for k in order:
        piece(k, 0, rows).wait_recv()


def propagate(field, wave_speed, substeps, east, north, neighbours, peers, spaces):
    rows, width = field.shape
    tiles = width // HALO
    reach = SUB * HALO
    assert width >= reach and spaces % 2 == 0
    chunk = chunk_rows(rows)
    block = math.gcd(tiles, 4)
    outer = tiles + 2 * SUB
    angles = (np.arange(ND, dtype=np.float32) + np.float32(0.5)) * np.float32(2.0 * math.pi / ND)
    trig = np.stack([np.cos(angles), np.sin(angles)])
    trig = np.ascontiguousarray(np.broadcast_to(trig[:, :, None], (2, ND, HALO)))
    vmem = pl.BlockSpec(memory_space=pltpu.VMEM)
    smem = pl.BlockSpec(memory_space=pltpu.SMEM)
    return pl.pallas_call(
        functools.partial(propagate_kernel, peers, spaces, chunk, block),
        out_shape=jax.ShapeDtypeStruct((peers * rows, HALO), jnp.float32),
        in_specs=[pl.BlockSpec(memory_space=pl.ANY), smem, smem, vmem, vmem, vmem, vmem],
        out_specs=vmem,
        scratch_shapes=[
            pltpu.VMEM((rows, width + 2 * reach), jnp.float32),
            pltpu.VMEM((tiles, rows, HALO), jnp.float32),
            pltpu.VMEM((2, 4, reach), jnp.int32),
            pltpu.VMEM((2, 2, 1, reach), jnp.float32),
            pltpu.VMEM((4, outer, 8, HALO), jnp.int32),
            pltpu.VMEM((2, outer, 8, HALO), jnp.float32),
            pltpu.SemaphoreType.DMA,
            pltpu.SemaphoreType.DMA((2, 3)),
            pltpu.SemaphoreType.DMA((2, 3)),
            pltpu.SemaphoreType.DMA((2,)),
            pltpu.SemaphoreType.DMA((2, rows // chunk)),
            pltpu.SemaphoreType.DMA((peers,)),
            pltpu.SemaphoreType.DMA((peers,)),
            pltpu.SemaphoreType.DMA,
            pltpu.SemaphoreType.REGULAR,
        ],
        compiler_params=pltpu.CompilerParams(collective_id=0, has_side_effects=True),
    )(
        field,
        wave_speed,
        substeps,
        jnp.asarray(trig),
        east.reshape(1, width),
        north.reshape(1, width),
        neighbours,
    )


def source_kernel(batch, quad_ref, strength_ref, points_ref, blocks_ref, out_ref, rounded, products):
    total = blocks_ref.shape[0]

    def fill(f, carry):
        value = points_ref[f]
        rounded[f] = value.astype(jnp.bfloat16)
        out_ref[f] = value
        return carry

    lax.fori_loop(0, NF, fill, 0, unroll=4)

    def step(i, carry):
        for b in range(batch):
            j = i * batch + b
            block = blocks_ref[j]
            left = jnp.dot(block, rounded[quad_ref[0, j]], preferred_element_type=jnp.float32)
            right = lax.dot_general(
                block,
                rounded[quad_ref[1, j]],
                (((0,), (0,)), ((), ())),
                preferred_element_type=jnp.float32,
            )
            products[b] = (left * right * points_ref[quad_ref[2, j]]).astype(jnp.bfloat16)
        parts = []
        for b in range(batch):
            j = i * batch + b
            part = jnp.dot(blocks_ref[j], products[b], preferred_element_type=jnp.float32)
            parts.append(part * (strength_ref[j] * source_step))
        for b in range(batch):
            target = quad_ref[3, i * batch + b]
            out_ref[target] = out_ref[target] + parts[b]
        return carry

    lax.fori_loop(0, total // batch, step, 0)


def source_term(points, blocks, quad_index, strength):
    width = points.shape[1]
    vmem = pl.BlockSpec(memory_space=pltpu.VMEM)
    smem = pl.BlockSpec(memory_space=pltpu.SMEM)
    batch = math.gcd(blocks.shape[0], 32)
    out = pl.pallas_call(
        functools.partial(source_kernel, batch),
        out_shape=jax.ShapeDtypeStruct((NF, ND, width), jnp.float32),
        in_specs=[smem, smem, vmem, vmem],
        out_specs=vmem,
        scratch_shapes=[
            pltpu.VMEM((NF, ND, width), jnp.bfloat16),
            pltpu.VMEM((batch, ND, width), jnp.bfloat16),
        ],
    )(quad_index, strength, points.reshape(NF, ND, width), blocks)
    return out.reshape(NF * ND, width)


def home_kernel(peers, points_ref, out_ref, send_sem, recv_sem, own_sem):
    me = lax.axis_index("comp")
    rows = out_ref.shape[0]
    place = pl.ds(pl.multiple_of(me * HALO, HALO), HALO)
    own = pltpu.make_async_copy(
        points_ref.at[pl.ds(pl.multiple_of(me * rows, 8), rows)], out_ref.at[:, place], own_sem
    )
    own.start()
    sync(peers, 0)
    copies = []
    for k in sorted(range(1, peers), key=lambda k: abs(k - peers / 2)):
        target = lax.rem(me + k, peers)
        copy = pltpu.make_async_remote_copy(
            src_ref=points_ref.at[pl.ds(pl.multiple_of(target * rows, 8), rows)],
            dst_ref=out_ref.at[:, place],
            send_sem=send_sem.at[k],
            recv_sem=recv_sem.at[k],
            device_id={"comp": target},
            device_id_type=MESH,
        )
        copy.start()
        copies.append(copy)
    own.wait()
    for copy in copies:
        copy.wait()


def send_home(points, peers):
    rows = points.shape[0] // peers
    return pl.pallas_call(
        functools.partial(home_kernel, peers),
        out_shape=jax.ShapeDtypeStruct((rows, peers * HALO), jnp.float32),
        in_specs=[pl.BlockSpec(memory_space=pltpu.VMEM)],
        out_specs=pl.BlockSpec(memory_space=pltpu.VMEM),
        scratch_shapes=[
            pltpu.SemaphoreType.DMA((peers,)),
            pltpu.SemaphoreType.DMA((peers,)),
            pltpu.SemaphoreType.DMA,
        ],
        compiler_params=pltpu.CompilerParams(collective_id=1, has_side_effects=True),
    )(points)


def shards(
    spectrum,
    wave_speed,
    current_east,
    current_north,
    substeps,
    neighbours,
    blocks,
    quad_index,
    strength,
):
    peers = lax.axis_size("comp")
    spaces = lax.axis_size("space")
    rows, width = spectrum.shape
    assert width == peers * HALO
    points = propagate(
        spectrum, wave_speed, substeps, current_east, current_north, neighbours, peers, spaces
    )
    points = source_term(points, blocks, quad_index, strength)
    return send_home(points, peers)


def solution(mesh):
    in_specs = (
        P("comp", ("grp", "space")),
        P(),
        P(("grp", "space")),
        P(("grp", "space")),
        P(),
        P(None, ("grp", "space")),
        P(),
        P(),
        P(),
    )
    out_specs = P("comp", ("grp", "space"))
    return jax.shard_map(shards, mesh=mesh, in_specs=in_specs, out_specs=out_specs, check_vma=False)
```

profile of v0, /device:TPU:9, one launch (start us, length us, event | category | flops | bytes accessed | tf_op | source)
XLA Modules:
  0.0 95.7 jit_solution(18392868583619528651)
XLA Ops:
  0.0 71.8 %shard_map.100 = f32[2304,128]{1,0:T(8,128)} custom-call(f32[576,512]{1,0:T(8,128)} %field_ref.1, f32[36]{0:T(128)} %wave_ref.1, s32[2304]{0:T(1024)} %substeps_ref.1, f32[2,64,128]{2,1,0:T(8,128)} %constant.2.clone.trig_ref, f32[1,512]{1,0:T(1,128)} %bitcast.6, f32[1,512]{1,0:T(1,128)} %bitcast.7, s32[4,512]{1,0:T(4,128)} %neighbour_ref.1), custom_call_target="tpu_custom_call" | custom-call | tf_op jit(solution)/shard_map/pallas_call | solution.py:387
  71.8 4.1 %shard_map.101 = f32[36,64,128]{2,1,0:T(8,128)} custom-call(s32[4,64]{1,0:T(4,128)} %quad_ref.1, f32[64]{0:T(128)} %strength_ref.1, f32[36,64,128]{2,1,0:T(8,128)} %bitcast.4, bf16[64,64,64]{2,1,0:T(8,128)(2,1)} %blocks_ref.1), custom_call_target="tpu_custom_call" | custom-call | tf_op jit(solution)/shard_map/pallas_call | solution.py:462
  75.9 17.4 %shard_map.102 = f32[576,512]{1,0:T(8,128)} custom-call(f32[2304,128]{1,0:T(8,128)} %bitcast.5), custom_call_target="tpu_custom_call" | custom-call | tf_op jit(solution)/shard_map/pallas_call | solution.py:504
  93.4 2.4 %copy.12 = f32[576,512]{1,0:T(8,128)} copy(f32[576,512]{1,0:T(8,128)} %shard_map.102) | data formatting | bytes 2359296
where the time goes:
time: 97.2 us; the launch traced here: 95.7 us
  Pallas kernels  93.3 us (96%)
  local copies, waits for them, and re-layouts  2.36 us (2%)
    pallas_call x1, Pallas kernels, propagate(): pl.pallas_call(functools.partial(propagate_kernel, peers, spaces, chunk,...  71.8 us
    pallas_call x1, Pallas kernels, send_home(): pl.pallas_call(functools.partial(home_kernel, peers), out_shape=jax.Shape...  17.4 us
    pallas_call x1, Pallas kernels, source_term(): pl.pallas_call(functools.partial(source_kernel, batch), out_shape=jax.Sha...  4.06 us
    unnamed x1, local copies, waits for them, and re-layouts  2.36 us

commit v1 on v0

--- a/solution.py
+++ b/solution.py
@@ -13,6 +13,7 @@
 ND = 64
 SUB = 4
 HALO = 128
+PARTS = 2
 
 courant_scale = 0.4
 courant_limit = 0.45
@@ -22,7 +23,7 @@
 
 
 def chunk_rows(rows):
-    for size in (32, 24, 16, 8):
+    for size in (64, 72, 48, 32, 24, 16, 8):
         if rows % size == 0:
             return size
     return rows
@@ -45,25 +46,6 @@
             )
             count += 1
     pl.semaphore_wait(barrier, count)
-
-
-GATHER = lax.GatherDimensionNumbers(
-    offset_dims=(),
-    collapsed_slice_dims=(1,),
-    start_index_map=(1,),
-    operand_batching_dims=(0,),
-    start_indices_batching_dims=(0,),
-)
-
-
-def take_lanes(values, index):
-    return lax.gather(
-        values,
-        index[:, :, None],
-        GATHER,
-        slice_sizes=(1, 1),
-        mode=lax.GatherScatterMode.PROMISE_IN_BOUNDS,
-    )
 
 
 def propagate_kernel(
@@ -83,8 +65,12 @@
     finals,
     side_table,
     side_current,
-    codes,
+    selector,
     currents,
+    states,
+    parts,
+    speeds,
+    repeats,
     load_sem,
     side_send,
     side_recv,
@@ -211,9 +197,14 @@
     def spread(row):
         return jnp.broadcast_to(row, (8, HALO))
 
+    spot = lax.broadcasted_iota(jnp.int32, (2 * HALO, HALO), 0)
+
     def fill(e, table_ref, east_row, north_row, tile, place):
         for d in range(4):
-            codes[d, e] = spread(table_ref[d : d + 1, place] - tile * HALO)
+            wanted = table_ref[d : d + 1, place] - (tile + d % 2) * HALO
+            half = d // 2 * HALO
+            chosen = jnp.where(spot == wanted, 1.0, 0.0).astype(jnp.bfloat16)
+            selector[e, d % 2, :, half : half + HALO] = chosen
         currents[0, e] = spread(east_row[:, place])
         currents[1, e] = spread(north_row[:, place])
 
@@ -243,48 +234,81 @@
     sublane = lax.broadcasted_iota(jnp.int32, (8, HALO), 0)
     window = block + 2 * SUB
 
-    def upwind(before, own, after, code, index):
-        picked = jnp.where(code >= 2 * HALO, take_lanes(after, index), take_lanes(own, index))
-        return jnp.where(code < HALO, take_lanes(before, index), picked)
-
-    def strip(row, b):
-        at = pl.ds(row, 8)
-        component = me * rows + row
-        speed = wave_ref[component // ND]
-        turn = pl.ds(pl.multiple_of(lax.rem(component, ND), 8), 8)
-        own_x = trig_ref[0, turn, :] * speed
-        own_y = trig_ref[1, turn, :] * speed
-        taken = jnp.full((8, HALO), substeps_ref[component], jnp.int32)
-        for i in range(1, 8):
-            taken = jnp.where(sublane == i, substeps_ref[component + i], taken)
-        scale = courant_scale / taken.astype(jnp.float32)
+    def prepare(first, base):
+        def per_group(g, carry):
+            at = pl.ds(pl.multiple_of(g * 8, 8), 8)
+            component = me * rows + first + g * 8
+            speed = wave_ref[component // ND]
+            turn = pl.ds(pl.multiple_of(lax.rem(component, ND), 8), 8)
+            own_x = trig_ref[0, turn, :] * speed
+            own_y = trig_ref[1, turn, :] * speed
+            taken = jnp.full((8, HALO), substeps_ref[component], jnp.int32)
+            for i in range(1, 8):
+                taken = jnp.where(sublane == i, substeps_ref[component + i], taken)
+            count = taken.astype(jnp.float32)
+            repeats[at] = count
+            scale = courant_scale / count
+            for i in range(1, window - 1):
+                along_x = (own_x + currents[0, base + i]) * scale
+                along_y = (own_y + currents[1, base + i]) * scale
+                speeds[0, i, at] = jnp.clip(along_x, -courant_limit, courant_limit)
+                speeds[1, i, at] = jnp.clip(along_y, -courant_limit, courant_limit)
+            return carry
+
+        lax.fori_loop(0, chunk // 8, per_group, 0)
+
+    stacked = chunk % 16 == 0
+
+    def pick(i, chosen):
+        if stacked:
+            pair = jnp.concatenate([parts[i], parts[i + 1]], axis=1)
+            both = jnp.dot(pair, chosen, preferred_element_type=jnp.float32)
+            taken = both[:chunk]
+            for p in range(1, PARTS):
+                taken = taken + both[p * chunk : (p + 1) * chunk]
+        else:
+            taken = None
+            for p in range(PARTS):
+                at = pl.ds(p * chunk, chunk)
+                pair = jnp.concatenate([parts[i, at], parts[i + 1, at]], axis=1)
+                term = jnp.dot(pair, chosen, preferred_element_type=jnp.float32)
+                taken = term if taken is None else taken + term
+        return taken[:, :HALO], taken[:, HALO:]
+
+    def advance(first, b):
         base = b * block
-        values = [
-            extended[at, pl.ds(pl.multiple_of((base + i) * HALO, HALO), HALO)] for i in range(window)
-        ]
-        along = {}
-        for i in range(1, window - 1):
-            entry = []
-            for axis, own in ((0, own_x), (1, own_y)):
-                moved = (own + currents[axis, base + i]) * scale
-                moved = jnp.clip(moved, -courant_limit, courant_limit)
-                code = jnp.where(moved > 0.0, codes[2 * axis, base + i], codes[2 * axis + 1, base + i])
-                entry.append((jnp.abs(moved), code, jnp.bitwise_and(code, HALO - 1)))
-            along[i] = entry
+        at = pl.ds(first, chunk)
+        prepare(first, base)
+
+        def state(s, i):
+            if s == 0:
+                return extended[at, pl.ds(pl.multiple_of((base + i) * HALO, HALO), HALO)]
+            return states[s % 2, i]
+
         for s in range(SUB):
-            latest = list(values)
+            for i in range(s, window - s):
+                rest = state(s, i)
+                for p in range(PARTS):
+                    part = rest.astype(jnp.bfloat16)
+                    parts[i, p * chunk : (p + 1) * chunk] = part
+                    if p + 1 < PARTS:
+                        rest = rest - part.astype(jnp.float32)
             for i in range(s + 1, window - 1 - s):
-                own = values[i]
-                change = None
-                for size, code, index in along[i]:
-                    term = size * (own - upwind(values[i - 1], own, values[i + 1], code, index))
-                    change = term if change is None else change + term
+                value = state(s, i)
+                west, south = pick(i - 1, selector[base + i, 0])
+                east, north = pick(i, selector[base + i, 1])
+                along_x = speeds[0, i]
+                along_y = speeds[1, i]
+                change = jnp.abs(along_x) * (value - jnp.where(along_x > 0.0, west, east))
+                change = change + jnp.abs(along_y) * (
+                    value - jnp.where(along_y > 0.0, south, north)
+                )
                 if s > 0:
-                    change = jnp.where(taken > s, change, 0.0)
-                latest[i] = own - change
-            values = latest
-        for i in range(block):
-            finals[base + i, at] = values[SUB + i]
+                    change = jnp.where(repeats[...] > float(s), change, 0.0)
+                if s + 1 < SUB:
+                    states[(s + 1) % 2, i] = value - change
+                else:
+                    finals[base + i - SUB, at] = value - change
 
     def piece(k, first, count):
         target = lax.rem(me + k, peers)
@@ -311,19 +335,14 @@
         def _():
             to_right.wait_recv()
 
-        def per_strip(g, inner):
-            row = pl.multiple_of(first + g * 8, 8)
-
-            def per_block(b, deepest):
-                strip(row, b)
-                return deepest
-
-            if tiles == block:
-                strip(row, 0)
-                return inner
-            return lax.fori_loop(0, tiles // block, per_block, inner)
-
-        lax.fori_loop(0, chunk // 8, per_strip, 0)
+        def per_block(b, inner):
+            advance(first, b)
+            return inner
+
+        if tiles == block:
+            advance(first, 0)
+        else:
+            lax.fori_loop(0, tiles // block, per_block, 0)
 
         @pl.when(goes_first)
         def _():
@@ -379,6 +398,7 @@
     chunk = chunk_rows(rows)
     block = math.gcd(tiles, 4)
     outer = tiles + 2 * SUB
+    window = block + 2 * SUB
     angles = (np.arange(ND, dtype=np.float32) + np.float32(0.5)) * np.float32(2.0 * math.pi / ND)
     trig = np.stack([np.cos(angles), np.sin(angles)])
     trig = np.ascontiguousarray(np.broadcast_to(trig[:, :, None], (2, ND, HALO)))
@@ -394,8 +414,12 @@
             pltpu.VMEM((tiles, rows, HALO), jnp.float32),
             pltpu.VMEM((2, 4, reach), jnp.int32),
             pltpu.VMEM((2, 2, 1, reach), jnp.float32),
-            pltpu.VMEM((4, outer, 8, HALO), jnp.int32),
+            pltpu.VMEM((outer, 2, 2 * HALO, 2 * HALO), jnp.bfloat16),
             pltpu.VMEM((2, outer, 8, HALO), jnp.float32),
+            pltpu.VMEM((2, window, chunk, HALO), jnp.float32),
+            pltpu.VMEM((window, PARTS * chunk, HALO), jnp.bfloat16),
+            pltpu.VMEM((2, window, chunk, HALO), jnp.float32),
+            pltpu.VMEM((chunk, HALO), jnp.float32),
             pltpu.SemaphoreType.DMA,
             pltpu.SemaphoreType.DMA((2, 3)),
             pltpu.SemaphoreType.DMA((2, 3)),

time: 97.2 us -> 71.4 us (0.73)
  Pallas kernels: 93.3 us -> 67.8 us
    pallas_call x1, Pallas kernels: 71.8 us -> 46.2 us  [propagate(): pl.pallas_call(functools.partial(propagate_kernel, peers, spaces, chunk,...]
where the time goes in v1:
time: 71.4 us; the launch traced here: 70.1 us
  Pallas kernels  67.8 us (95%)
  local copies, waits for them, and re-layouts  2.36 us (3%)
    pallas_call x1, Pallas kernels, propagate(): pl.pallas_call(functools.partial(propagate_kernel, peers, spaces, chunk,...  46.2 us
    pallas_call x1, Pallas kernels, send_home(): pl.pallas_call(functools.partial(home_kernel, peers), out_shape=jax.Shape...  17.4 us
    pallas_call x1, Pallas kernels, source_term(): pl.pallas_call(functools.partial(source_kernel, batch), out_shape=jax.Sha...  4.06 us
    unnamed x1, local copies, waits for them, and re-layouts  2.36 us

profile of v1, /device:TPU:9, one launch (start us, length us, event | category | flops | bytes accessed | tf_op | source)
XLA Modules:
  0.0 70.1 jit_solution(13569351850998898812)
XLA Ops:
  0.0 46.2 %shard_map.100 = f32[2304,128]{1,0:T(8,128)} custom-call(f32[576,512]{1,0:T(8,128)} %field_ref.1, f32[36]{0:T(128)} %wave_ref.1, s32[2304]{0:T(1024)} %substeps_ref.1, f32[2,64,128]{2,1,0:T(8,128)} %constant.2.clone.trig_ref, f32[1,512]{1,0:T(1,128)} %bitcast.6, f32[1,512]{1,0:T(1,128)} %bitcast.7, s32[4,512]{1,0:T(4,128)} %neighbour_ref.1), custom_call_target="tpu_custom_call" | custom-call | tf_op jit(solution)/shard_map/pallas_call | solution.py:407
  46.3 4.1 %shard_map.101 = f32[36,64,128]{2,1,0:T(8,128)} custom-call(s32[4,64]{1,0:T(4,128)} %quad_ref.1, f32[64]{0:T(128)} %strength_ref.1, f32[36,64,128]{2,1,0:T(8,128)} %bitcast.4, bf16[64,64,64]{2,1,0:T(8,128)(2,1)} %blocks_ref.1), custom_call_target="tpu_custom_call" | custom-call | tf_op jit(solution)/shard_map/pallas_call | solution.py:486
  50.3 17.4 %shard_map.102 = f32[576,512]{1,0:T(8,128)} custom-call(f32[2304,128]{1,0:T(8,128)} %bitcast.5), custom_call_target="tpu_custom_call" | custom-call | tf_op jit(solution)/shard_map/pallas_call | solution.py:528
  67.8 2.4 %copy.12 = f32[576,512]{1,0:T(8,128)} copy(f32[576,512]{1,0:T(8,128)} %shard_map.102) | data formatting | bytes 2359296

commit v2 on v1

--- a/solution.py
+++ b/solution.py
@@ -14,6 +14,7 @@
 SUB = 4
 HALO = 128
 PARTS = 2
+EARLY = 0
 
 courant_scale = 0.4
 courant_limit = 0.45
@@ -48,11 +49,13 @@
     pl.semaphore_wait(barrier, count)
 
 
-def propagate_kernel(
+def wave_kernel(
     peers,
     spaces,
     chunk,
     block,
+    batch,
+    early,
     field_ref,
     wave_ref,
     substeps_ref,
@@ -60,6 +63,10 @@
     east_ref,
     north_ref,
     neighbour_ref,
+    quad_ref,
+    strength_ref,
+    blocks_ref,
+    out_ref,
     points_ref,
     extended,
     finals,
@@ -71,13 +78,25 @@
     parts,
     speeds,
     repeats,
+    links,
+    chain,
+    blocks,
+    fields,
+    rounded,
+    products,
+    slots,
+    updated,
     load_sem,
+    blocks_sem,
+    chain_sem,
     side_send,
     side_recv,
     halo_send,
     halo_recv,
     piece_send,
     piece_recv,
+    home_send,
+    home_recv,
     own_sem,
     turn_sem,
 ):
@@ -94,6 +113,8 @@
 
     load = pltpu.make_async_copy(field_ref, extended.at[:, pl.ds(reach, width)], load_sem)
     load.start()
+    load_blocks = pltpu.make_async_copy(blocks_ref, blocks, blocks_sem)
+    load_blocks.start()
 
     sync(peers, spaces)
 
@@ -213,6 +234,28 @@
         return carry
 
     lax.fori_loop(0, tiles, fill_own, 0)
+
+    total = blocks.shape[0]
+    spots = lax.broadcasted_iota(jnp.int32, (1, HALO), 1)
+    none = jnp.full((1, HALO), total, jnp.int32)
+
+    def targets(j, row):
+        return jnp.where(spots == j, quad_ref[3, j], row)
+
+    def link(j, carry):
+        before, last = carry
+        target = quad_ref[3, j]
+        before = jnp.where(jnp.logical_and(spots > j, row == target), j, before)
+        last = jnp.where(spots == target, j, last)
+        return before, last
+
+    row = lax.fori_loop(0, total, targets, none)
+    before, last = lax.fori_loop(0, total, link, (none, none))
+    links[0:1] = before
+    links[1:2] = last
+    load_chain = pltpu.make_async_copy(links, chain, chain_sem)
+    load_chain.start()
+    slots[total] = jnp.zeros((ND, HALO), jnp.float32)
 
     @pl.when(has_right)
     def _():
@@ -344,7 +387,7 @@
         else:
             lax.fori_loop(0, tiles // block, per_block, 0)
 
-        @pl.when(goes_first)
+        @pl.when(jnp.logical_or(goes_first, c < early))
         def _():
             for k in order:
                 piece(k, first, chunk).start()
@@ -352,26 +395,95 @@
         return carry
 
     lax.fori_loop(0, chunks, step, 0)
-    own = pltpu.make_async_copy(
-        finals.at[me], points_ref.at[pl.ds(pl.multiple_of(me * rows, 8), rows)], own_sem
-    )
+    place = pl.ds(pl.multiple_of(me * rows, 8), rows)
+    own = pltpu.make_async_copy(finals.at[me], points_ref.at[place], own_sem)
     own.start()
 
     @pl.when(jnp.logical_not(goes_first))
     def _():
-        pl.semaphore_wait(turn_sem, 1)
-        for k in order:
-            piece(k, 0, rows).start()
+        pl.semaphore_wait(turn_sem.at[0], 1)
+        if early < chunks:
+            for k in order:
+                piece(k, early * chunk, rows - early * chunk).start()
 
     for k in order:
         piece(k, 0, rows).wait_send()
+    partner = {"space": here + 1 - 2 * odd}
 
     @pl.when(goes_first)
     def _():
-        partner = here + 1 - 2 * odd
-        pl.semaphore_signal(turn_sem, inc=1, device_id={"space": partner}, device_id_type=MESH)
+        pl.semaphore_signal(turn_sem.at[0], inc=1, device_id=partner, device_id_type=MESH)
+
+    @pl.when(jnp.logical_not(goes_first))
+    def _():
+        pl.semaphore_signal(turn_sem.at[1], inc=1, device_id=partner, device_id_type=MESH)
 
     own.wait()
+    load_blocks.wait()
+    load_chain.wait()
+    for k in order:
+        piece(k, 0, rows).wait_recv()
+
+    def frequency(f):
+        return pl.ds(pl.multiple_of(f * ND, ND), ND)
+
+    def take(f, carry):
+        value = points_ref[frequency(f)]
+        rounded[f] = value.astype(jnp.bfloat16)
+        fields[f] = value
+        return carry
+
+    lax.fori_loop(0, NF, take, 0, unroll=4)
+
+    def interact(i, carry):
+        for b in range(batch):
+            j = i * batch + b
+            matrix = blocks[j]
+            left_term = jnp.dot(matrix, rounded[quad_ref[0, j]], preferred_element_type=jnp.float32)
+            right_term = lax.dot_general(
+                matrix,
+                rounded[quad_ref[1, j]],
+                (((0,), (0,)), ((), ())),
+                preferred_element_type=jnp.float32,
+            )
+            products[b] = (left_term * right_term * fields[quad_ref[2, j]]).astype(jnp.bfloat16)
+        terms = []
+        for b in range(batch):
+            j = i * batch + b
+            term = jnp.dot(blocks[j], products[b], preferred_element_type=jnp.float32)
+            terms.append(term * (strength_ref[j] * source_step))
+        for b in range(batch):
+            j = i * batch + b
+            slots[j] = slots[chain[0, j]] + terms[b]
+        return carry
+
+    lax.fori_loop(0, total // batch, interact, 0)
+
+    def finish(f, carry):
+        updated[frequency(f)] = fields[f] + slots[chain[1, f]]
+        return carry
+
+    lax.fori_loop(0, NF, finish, 0, unroll=4)
+
+    @pl.when(goes_first)
+    def _():
+        pl.semaphore_wait(turn_sem.at[1], 1)
+
+    column = pl.ds(pl.multiple_of(me * HALO, HALO), HALO)
+    homes = []
+    for k in order:
+        target = lax.rem(me + k, peers)
+        home = remote(
+            updated.at[pl.ds(pl.multiple_of(target * rows, 8), rows)],
+            out_ref.at[:, column],
+            home_send.at[k],
+            home_recv.at[k],
+            {"comp": target},
+        )
+        home.start()
+        homes.append(home)
+    own = pltpu.make_async_copy(updated.at[place], out_ref.at[:, column], own_sem)
+    own.start()
     to_left, to_right = halo(0, rows, 0)
 
     @pl.when(has_left)
@@ -386,30 +498,38 @@
         for copy in to_right_sides:
             copy.wait_send()
 
-    for k in order:
-        piece(k, 0, rows).wait_recv()
-
-
-def propagate(field, wave_speed, substeps, east, north, neighbours, peers, spaces):
+    own.wait()
+    for home in homes:
+        home.wait()
+
+
+def advance_waves(
+    field, wave_speed, substeps, east, north, neighbours, blocks, quad_index, strength, peers, spaces
+):
     rows, width = field.shape
     tiles = width // HALO
     reach = SUB * HALO
-    assert width >= reach and spaces % 2 == 0
+    total = blocks.shape[0]
+    assert width >= reach and spaces % 2 == 0 and max(total, NF) < HALO
     chunk = chunk_rows(rows)
     block = math.gcd(tiles, 4)
     outer = tiles + 2 * SUB
     window = block + 2 * SUB
+    batch = math.gcd(total, 32)
+    early = min(EARLY, rows // chunk)
     angles = (np.arange(ND, dtype=np.float32) + np.float32(0.5)) * np.float32(2.0 * math.pi / ND)
     trig = np.stack([np.cos(angles), np.sin(angles)])
     trig = np.ascontiguousarray(np.broadcast_to(trig[:, :, None], (2, ND, HALO)))
     vmem = pl.BlockSpec(memory_space=pltpu.VMEM)
     smem = pl.BlockSpec(memory_space=pltpu.SMEM)
+    whole = pl.BlockSpec(memory_space=pl.ANY)
     return pl.pallas_call(
-        functools.partial(propagate_kernel, peers, spaces, chunk, block),
-        out_shape=jax.ShapeDtypeStruct((peers * rows, HALO), jnp.float32),
-        in_specs=[pl.BlockSpec(memory_space=pl.ANY), smem, smem, vmem, vmem, vmem, vmem],
-        out_specs=vmem,
+        functools.partial(wave_kernel, peers, spaces, chunk, block, batch, early),
+        out_shape=jax.ShapeDtypeStruct((rows, width), jnp.float32),
+        in_specs=[whole, smem, smem, vmem, vmem, vmem, vmem, smem, smem, whole],
+        out_specs=whole,
         scratch_shapes=[
+            pltpu.VMEM((peers * rows, HALO), jnp.float32),
             pltpu.VMEM((rows, width + 2 * reach), jnp.float32),
             pltpu.VMEM((tiles, rows, HALO), jnp.float32),
             pltpu.VMEM((2, 4, reach), jnp.int32),
@@ -420,6 +540,16 @@
             pltpu.VMEM((window, PARTS * chunk, HALO), jnp.bfloat16),
             pltpu.VMEM((2, window, chunk, HALO), jnp.float32),
             pltpu.VMEM((chunk, HALO), jnp.float32),
+            pltpu.VMEM((8, HALO), jnp.int32),
+            pltpu.SMEM((8, HALO), jnp.int32),
+            pltpu.VMEM(blocks.shape, jnp.bfloat16),
+            pltpu.VMEM((NF, ND, HALO), jnp.float32),
+            pltpu.VMEM((NF, ND, HALO), jnp.bfloat16),
+            pltpu.VMEM((batch, ND, HALO), jnp.bfloat16),
+            pltpu.VMEM((total + 1, ND, HALO), jnp.float32),
+            pltpu.VMEM((peers * rows, HALO), jnp.float32),
+            pltpu.SemaphoreType.DMA,
+            pltpu.SemaphoreType.DMA,
             pltpu.SemaphoreType.DMA,
             pltpu.SemaphoreType.DMA((2, 3)),
             pltpu.SemaphoreType.DMA((2, 3)),
@@ -427,8 +557,10 @@
             pltpu.SemaphoreType.DMA((2, rows // chunk)),
             pltpu.SemaphoreType.DMA((peers,)),
             pltpu.SemaphoreType.DMA((peers,)),
+            pltpu.SemaphoreType.DMA((peers,)),
+            pltpu.SemaphoreType.DMA((peers,)),
             pltpu.SemaphoreType.DMA,
-            pltpu.SemaphoreType.REGULAR,
+            pltpu.SemaphoreType.REGULAR((2,)),
         ],
         compiler_params=pltpu.CompilerParams(collective_id=0, has_side_effects=True),
     )(
@@ -439,104 +571,10 @@
         east.reshape(1, width),
         north.reshape(1, width),
         neighbours,
+        quad_index,
+        strength,
+        blocks,
     )
-
-
-def source_kernel(batch, quad_ref, strength_ref, points_ref, blocks_ref, out_ref, rounded, products):
-    total = blocks_ref.shape[0]
-
-    def fill(f, carry):
-        value = points_ref[f]
-        rounded[f] = value.astype(jnp.bfloat16)
-        out_ref[f] = value
-        return carry
-
-    lax.fori_loop(0, NF, fill, 0, unroll=4)
-
-    def step(i, carry):
-        for b in range(batch):
-            j = i * batch + b
-            block = blocks_ref[j]
-            left = jnp.dot(block, rounded[quad_ref[0, j]], preferred_element_type=jnp.float32)
-            right = lax.dot_general(
-                block,
-                rounded[quad_ref[1, j]],
-                (((0,), (0,)), ((), ())),
-                preferred_element_type=jnp.float32,
-            )
-            products[b] = (left * right * points_ref[quad_ref[2, j]]).astype(jnp.bfloat16)
-        parts = []
-        for b in range(batch):
-            j = i * batch + b
-            part = jnp.dot(blocks_ref[j], products[b], preferred_element_type=jnp.float32)
-            parts.append(part * (strength_ref[j] * source_step))
-        for b in range(batch):
-            target = quad_ref[3, i * batch + b]
-            out_ref[target] = out_ref[target] + parts[b]
-        return carry
-
-    lax.fori_loop(0, total // batch, step, 0)
-
-
-def source_term(points, blocks, quad_index, strength):
-    width = points.shape[1]
-    vmem = pl.BlockSpec(memory_space=pltpu.VMEM)
-    smem = pl.BlockSpec(memory_space=pltpu.SMEM)
-    batch = math.gcd(blocks.shape[0], 32)
-    out = pl.pallas_call(
-        functools.partial(source_kernel, batch),
-        out_shape=jax.ShapeDtypeStruct((NF, ND, width), jnp.float32),
-        in_specs=[smem, smem, vmem, vmem],
-        out_specs=vmem,
-        scratch_shapes=[
-            pltpu.VMEM((NF, ND, width), jnp.bfloat16),
-            pltpu.VMEM((batch, ND, width), jnp.bfloat16),
-        ],
-    )(quad_index, strength, points.reshape(NF, ND, width), blocks)
-    return out.reshape(NF * ND, width)
-
-
-def home_kernel(peers, points_ref, out_ref, send_sem, recv_sem, own_sem):
-    me = lax.axis_index("comp")
-    rows = out_ref.shape[0]
-    place = pl.ds(pl.multiple_of(me * HALO, HALO), HALO)
-    own = pltpu.make_async_copy(
-        points_ref.at[pl.ds(pl.multiple_of(me * rows, 8), rows)], out_ref.at[:, place], own_sem
-    )
-    own.start()
-    sync(peers, 0)
-    copies = []
-    for k in sorted(range(1, peers), key=lambda k: abs(k - peers / 2)):
-        target = lax.rem(me + k, peers)
-        copy = pltpu.make_async_remote_copy(
-            src_ref=points_ref.at[pl.ds(pl.multiple_of(target * rows, 8), rows)],
-            dst_ref=out_ref.at[:, place],
-            send_sem=send_sem.at[k],
-            recv_sem=recv_sem.at[k],
-            device_id={"comp": target},
-            device_id_type=MESH,
-        )
-        copy.start()
-        copies.append(copy)
-    own.wait()
-    for copy in copies:
-        copy.wait()
-
-
-def send_home(points, peers):
-    rows = points.shape[0] // peers
-    return pl.pallas_call(
-        functools.partial(home_kernel, peers),
-        out_shape=jax.ShapeDtypeStruct((rows, peers * HALO), jnp.float32),
-        in_specs=[pl.BlockSpec(memory_space=pltpu.VMEM)],
-        out_specs=pl.BlockSpec(memory_space=pltpu.VMEM),
-        scratch_shapes=[
-            pltpu.SemaphoreType.DMA((peers,)),
-            pltpu.SemaphoreType.DMA((peers,)),
-            pltpu.SemaphoreType.DMA,
-        ],
-        compiler_params=pltpu.CompilerParams(collective_id=1, has_side_effects=True),
-    )(points)
 
 
 def shards(
@@ -554,11 +592,19 @@
     spaces = lax.axis_size("space")
     rows, width = spectrum.shape
     assert width == peers * HALO
-    points = propagate(
-        spectrum, wave_speed, substeps, current_east, current_north, neighbours, peers, spaces
+    return advance_waves(
+        spectrum,
+        wave_speed,
+        substeps,
+        current_east,
+        current_north,
+        neighbours,
+        blocks,
+        quad_index,
+        strength,
+        peers,
+        spaces,
     )
-    points = source_term(points, blocks, quad_index, strength)
-    return send_home(points, peers)
 
 
 def solution(mesh):

time: 71.4 us -> 65.3 us (0.915); the launches traced: 70.1 us -> 65.1 us
  Pallas kernels: 67.8 us -> 62.7 us
    pallas_call x3 -> x1, Pallas kernels: 67.8 us -> 62.7 us  [advance_waves(): pl.pallas_call(functools.partial(wave_kernel, peers, spaces, chunk, block...]
where the time goes in v2:
time: 65.3 us; the launch traced here: 65.1 us
  Pallas kernels  62.7 us (96%)
  local copies, waits for them, and re-layouts  2.36 us (4%)
    pallas_call x1, Pallas kernels, advance_waves(): pl.pallas_call(functools.partial(wave_kernel, peers, spaces, chunk, block...  62.7 us
    unnamed x1, local copies, waits for them, and re-layouts  2.36 us

profile of v2, /device:TPU:9, one launch (start us, length us, event | category | flops | bytes accessed | tf_op | source)
XLA Modules:
  0.0 65.1 jit_solution(14511172813772168582)
XLA Ops:
  0.0 62.7 %shard_map.100 = f32[576,512]{1,0:T(8,128)} custom-call(f32[576,512]{1,0:T(8,128)} %field_ref.1, f32[36]{0:T(128)} %wave_ref.1, s32[2304]{0:T(1024)} %substeps_ref.1, f32[2,64,128]{2,1,0:T(8,128)} %constant.2.clone.trig_ref, f32[1,512]{1,0:T(1,128)} %bitcast.2, f32[1,512]{1,0:T(1,128)} %bitcast.3, s32[4,512]{1,0:T(4,128)} %neighbour_ref.1, ...), custom_call_target="tpu_custom_call" | custom-call | tf_op jit(solution)/shard_map/pallas_call | solution.py:526
  62.7 2.4 %copy.12 = f32[576,512]{1,0:T(8,128)} copy(f32[576,512]{1,0:T(8,128)} %shard_map.100) | data formatting | bytes 2359296

commit v3 on v2

--- a/solution.py
+++ b/solution.py
@@ -14,7 +14,8 @@
 SUB = 4
 HALO = 128
 PARTS = 2
-EARLY = 0
+EARLY = 2
+LATE = 2
 
 courant_scale = 0.4
 courant_limit = 0.45
@@ -30,7 +31,7 @@
     return rows
 
 
-def sync(peers, spaces):
+def greet(peers, spaces):
     me = lax.axis_index("comp")
     here = lax.axis_index("space")
     barrier = pltpu.get_barrier_semaphore()
@@ -40,13 +41,12 @@
             barrier, inc=1, device_id={"comp": lax.rem(me + k, peers)}, device_id_type=MESH
         )
         count += 1
-    if spaces:
-        for k in (1, spaces - 1):
-            pl.semaphore_signal(
-                barrier, inc=1, device_id={"space": lax.rem(here + k, spaces)}, device_id_type=MESH
-            )
-            count += 1
-    pl.semaphore_wait(barrier, count)
+    for k in (1, spaces - 1):
+        pl.semaphore_signal(
+            barrier, inc=1, device_id={"space": lax.rem(here + k, spaces)}, device_id_type=MESH
+        )
+        count += 1
+    return barrier, count
 
 
 def wave_kernel(
@@ -56,6 +56,7 @@
     block,
     batch,
     early,
+    late,
     field_ref,
     wave_ref,
     substeps_ref,
@@ -116,7 +117,69 @@
     load_blocks = pltpu.make_async_copy(blocks_ref, blocks, blocks_sem)
     load_blocks.start()
 
-    sync(peers, spaces)
+    barrier, greetings = greet(peers, spaces)
+    lane = lax.broadcasted_iota(jnp.int32, (4, HALO), 1)
+    for side, missing in ((0, jnp.logical_not(has_left)), (1, jnp.logical_not(has_right))):
+
+        @pl.when(missing)
+        def _(side=side):
+            first = (tiles - SUB) * HALO if side == 0 else 0
+            for i in range(SUB):
+                part = pl.ds(i * HALO, HALO)
+                side_table[side, :, part] = lane + (first + (i + 1) * HALO)
+            side_current[side] = jnp.zeros((2, 1, reach), jnp.float32)
+            start = 0 if side == 0 else reach + width
+
+            def clear(g, carry):
+                at = pl.ds(pl.multiple_of(g * 8, 8), 8)
+                extended[at, pl.ds(start, reach)] = jnp.zeros((8, reach), jnp.float32)
+                return carry
+
+            lax.fori_loop(0, rows // 8, clear, 0)
+
+    def spread(row):
+        return jnp.broadcast_to(row, (8, HALO))
+
+    spot = lax.broadcasted_iota(jnp.int32, (2 * HALO, HALO), 0)
+
+    def fill(e, table_ref, east_row, north_row, tile, place):
+        for d in range(4):
+            wanted = table_ref[d : d + 1, place] - (tile + d % 2) * HALO
+            half = d // 2 * HALO
+            chosen = jnp.where(spot == wanted, 1.0, 0.0).astype(jnp.bfloat16)
+            selector[e, d % 2, :, half : half + HALO] = chosen
+        currents[0, e] = spread(east_row[:, place])
+        currents[1, e] = spread(north_row[:, place])
+
+    def fill_own(j, carry):
+        fill(j + SUB, neighbour_ref, east_ref, north_ref, j, pl.ds(pl.multiple_of(j * HALO, HALO), HALO))
+        return carry
+
+    lax.fori_loop(0, tiles, fill_own, 0)
+
+    total = blocks.shape[0]
+    spots = lax.broadcasted_iota(jnp.int32, (1, HALO), 1)
+    none = jnp.full((1, HALO), total, jnp.int32)
+
+    def targets(j, row):
+        return jnp.where(spots == j, quad_ref[3, j], row)
+
+    def link(j, carry):
+        before, last = carry
+        target = quad_ref[3, j]
+        before = jnp.where(jnp.logical_and(spots > j, row == target), j, before)
+        last = jnp.where(spots == target, j, last)
+        return before, last
+
+    row = lax.fori_loop(0, total, targets, none)
+    before, last = lax.fori_loop(0, total, link, (none, none))
+    links[0:1] = before
+    links[1:2] = last
+    load_chain = pltpu.make_async_copy(links, chain, chain_sem)
+    load_chain.start()
+    slots[total] = jnp.zeros((ND, HALO), jnp.float32)
+
+    pl.semaphore_wait(barrier, greetings)
 
     left = {"space": jnp.maximum(here - 1, 0)}
     right = {"space": jnp.minimum(here + 1, spaces - 1)}
@@ -195,67 +258,6 @@
         return carry
 
     lax.fori_loop(0, chunks, start_halo, 0)
-
-    lane = lax.broadcasted_iota(jnp.int32, (4, HALO), 1)
-    for side, missing in ((0, jnp.logical_not(has_left)), (1, jnp.logical_not(has_right))):
-
-        @pl.when(missing)
-        def _(side=side):
-            first = (tiles - SUB) * HALO if side == 0 else 0
-            for i in range(SUB):
-                part = pl.ds(i * HALO, HALO)
-                side_table[side, :, part] = lane + (first + (i + 1) * HALO)
-            side_current[side] = jnp.zeros((2, 1, reach), jnp.float32)
-            start = 0 if side == 0 else reach + width
-
-            def clear(g, carry):
-                at = pl.ds(pl.multiple_of(g * 8, 8), 8)
-                extended[at, pl.ds(start, reach)] = jnp.zeros((8, reach), jnp.float32)
-                return carry
-
-            lax.fori_loop(0, rows // 8, clear, 0)
-
-    def spread(row):
-        return jnp.broadcast_to(row, (8, HALO))
-
-    spot = lax.broadcasted_iota(jnp.int32, (2 * HALO, HALO), 0)
-
-    def fill(e, table_ref, east_row, north_row, tile, place):
-        for d in range(4):
-            wanted = table_ref[d : d + 1, place] - (tile + d % 2) * HALO
-            half = d // 2 * HALO
-            chosen = jnp.where(spot == wanted, 1.0, 0.0).astype(jnp.bfloat16)
-            selector[e, d % 2, :, half : half + HALO] = chosen
-        currents[0, e] = spread(east_row[:, place])
-        currents[1, e] = spread(north_row[:, place])
-
-    def fill_own(j, carry):
-        fill(j + SUB, neighbour_ref, east_ref, north_ref, j, pl.ds(pl.multiple_of(j * HALO, HALO), HALO))
-        return carry
-
-    lax.fori_loop(0, tiles, fill_own, 0)
-
-    total = blocks.shape[0]
-    spots = lax.broadcasted_iota(jnp.int32, (1, HALO), 1)
-    none = jnp.full((1, HALO), total, jnp.int32)
-
-    def targets(j, row):
-        return jnp.where(spots == j, quad_ref[3, j], row)
-
-    def link(j, carry):
-        before, last = carry
-        target = quad_ref[3, j]
-        before = jnp.where(jnp.logical_and(spots > j, row == target), j, before)
-        last = jnp.where(spots == target, j, last)
-        return before, last
-
-    row = lax.fori_loop(0, total, targets, none)
-    before, last = lax.fori_loop(0, total, link, (none, none))
-    links[0:1] = before
-    links[1:2] = last
-    load_chain = pltpu.make_async_copy(links, chain, chain_sem)
-    load_chain.start()
-    slots[total] = jnp.zeros((ND, HALO), jnp.float32)
 
     @pl.when(has_right)
     def _():
@@ -353,12 +355,12 @@
                 else:
                     finals[base + i - SUB, at] = value - change
 
-    def piece(k, first, count):
+    def piece(k, first, count, group):
         target = lax.rem(me + k, peers)
         return remote(
             finals.at[target, pl.ds(first, count)],
             points_ref.at[pl.ds(pl.multiple_of(me * rows + first, 8), count)],
-            piece_send.at[k],
+            piece_send.at[group, k],
             piece_recv.at[k],
             {"comp": target},
         )
@@ -390,7 +392,7 @@
         @pl.when(jnp.logical_or(goes_first, c < early))
         def _():
             for k in order:
-                piece(k, first, chunk).start()
+                piece(k, first, chunk, jnp.where(c < chunks - late, 0, 1)).start()
 
         return carry
 
@@ -398,16 +400,20 @@
     place = pl.ds(pl.multiple_of(me * rows, 8), rows)
     own = pltpu.make_async_copy(finals.at[me], points_ref.at[place], own_sem)
     own.start()
+    most = (chunks - late) * chunk
 
     @pl.when(jnp.logical_not(goes_first))
     def _():
         pl.semaphore_wait(turn_sem.at[0], 1)
-        if early < chunks:
+        if early < chunks - late:
             for k in order:
-                piece(k, early * chunk, rows - early * chunk).start()
+                piece(k, early * chunk, most - early * chunk, 0).start()
+        if late:
+            for k in order:
+                piece(k, most, rows - most, 1).start()
 
     for k in order:
-        piece(k, 0, rows).wait_send()
+        piece(k, 0, most, 0).wait_send()
     partner = {"space": here + 1 - 2 * odd}
 
     @pl.when(goes_first)
@@ -422,7 +428,7 @@
     load_blocks.wait()
     load_chain.wait()
     for k in order:
-        piece(k, 0, rows).wait_recv()
+        piece(k, 0, rows, 0).wait_recv()
 
     def frequency(f):
         return pl.ds(pl.multiple_of(f * ND, ND), ND)
@@ -499,6 +505,9 @@
             copy.wait_send()
 
     own.wait()
+    if late:
+        for k in order:
+            piece(k, most, rows - most, 1).wait_send()
     for home in homes:
         home.wait()
 
@@ -516,7 +525,8 @@
     outer = tiles + 2 * SUB
     window = block + 2 * SUB
     batch = math.gcd(total, 32)
-    early = min(EARLY, rows // chunk)
+    late = min(LATE, rows // chunk - 1)
+    early = min(EARLY, rows // chunk - late)
     angles = (np.arange(ND, dtype=np.float32) + np.float32(0.5)) * np.float32(2.0 * math.pi / ND)
     trig = np.stack([np.cos(angles), np.sin(angles)])
     trig = np.ascontiguousarray(np.broadcast_to(trig[:, :, None], (2, ND, HALO)))
@@ -524,10 +534,10 @@
     smem = pl.BlockSpec(memory_space=pltpu.SMEM)
     whole = pl.BlockSpec(memory_space=pl.ANY)
     return pl.pallas_call(
-        functools.partial(wave_kernel, peers, spaces, chunk, block, batch, early),
-        out_shape=jax.ShapeDtypeStruct((rows, width), jnp.float32),
+        functools.partial(wave_kernel, peers, spaces, chunk, block, batch, early, late),
+        out_shape=pltpu.VMEM((rows, width), jnp.float32),
         in_specs=[whole, smem, smem, vmem, vmem, vmem, vmem, smem, smem, whole],
-        out_specs=whole,
+        out_specs=vmem,
         scratch_shapes=[
             pltpu.VMEM((peers * rows, HALO), jnp.float32),
             pltpu.VMEM((rows, width + 2 * reach), jnp.float32),
@@ -555,7 +565,7 @@
             pltpu.SemaphoreType.DMA((2, 3)),
             pltpu.SemaphoreType.DMA((2,)),
             pltpu.SemaphoreType.DMA((2, rows // chunk)),
-            pltpu.SemaphoreType.DMA((peers,)),
+            pltpu.SemaphoreType.DMA((2, peers)),
             pltpu.SemaphoreType.DMA((peers,)),
             pltpu.SemaphoreType.DMA((peers,)),
             pltpu.SemaphoreType.DMA((peers,)),

time: 65.3 us -> 61.1 us (0.936)
  Pallas kernels: 62.7 us -> 59.9 us
  local copies, waits for them, and re-layouts: 2.36 us -> 1.02 us
    pallas_call x1, Pallas kernels: 62.7 us -> 59.9 us  [advance_waves(): pl.pallas_call(functools.partial(wave_kernel, peers, spaces, chunk, block...]
    unnamed x1, local copies, waits for them, and re-layouts: 2.36 us -> 1.02 us
where the time goes in v3:
time: 61.1 us; the launch traced here: 60.9 us
  Pallas kernels  59.9 us (98%)
  local copies, waits for them, and re-layouts  1.02 us (2%)
    pallas_call x1, Pallas kernels, advance_waves(): pl.pallas_call(functools.partial(wave_kernel, peers, spaces, chunk, block...  59.9 us

profile of v3, /device:TPU:9, one launch (start us, length us, event | category | flops | bytes accessed | tf_op | source)
XLA Modules:
  0.0 60.9 jit_solution(18407930251303124777)
XLA Ops:
  0.0 59.9 %shard_map.100 = f32[576,512]{1,0:T(8,128)S(1)} custom-call(f32[576,512]{1,0:T(8,128)} %field_ref.1, f32[36]{0:T(128)} %wave_ref.1, s32[2304]{0:T(1024)} %substeps_ref.1, f32[2,64,128]{2,1,0:T(8,128)} %constant.2.clone.trig_ref, f32[1,512]{1,0:T(1,128)} %bitcast.2, f32[1,512]{1,0:T(1,128)} %bitcast.3, s32[4,512]{1,0:T(4,128)} %neighbour_ref.1, ...), custom_call_target="tpu_custom_call" | custom-call | tf_op jit(solution)/shard_map/pallas_call | solution.py:536
  59.9 1.0 %copy.12 = f32[576,512]{1,0:T(8,128)} copy(f32[576,512]{1,0:T(8,128)S(1)} %shard_map.100) | data formatting | bytes 2359296

commit v4 on v3

--- a/solution.py
+++ b/solution.py
@@ -15,7 +15,8 @@
 HALO = 128
 PARTS = 2
 EARLY = 2
-LATE = 2
+LATE_FIRST = 2
+LATE_SECOND = 4
 
 courant_scale = 0.4
 courant_limit = 0.45
@@ -36,17 +37,71 @@
     here = lax.axis_index("space")
     barrier = pltpu.get_barrier_semaphore()
     count = 0
-    for k in range(1, peers):
+    for axis, place, size in (("comp", me, peers), ("space", here, spaces)):
+        for step, near in ((-1, place > 0), (1, place < size - 1)):
+
+            @pl.when(near)
+            def _(axis=axis, place=place, step=step):
+                pl.semaphore_signal(
+                    barrier, inc=1, device_id={axis: place + step}, device_id_type=MESH
+                )
+
+            count = count + jnp.where(near, 1, 0)
+    return barrier, count
+
+
+def pass_word(peers, word_sem):
+    me = lax.axis_index("comp")
+
+    def onward(side, waits, step):
+        @pl.when(waits)
+        def _():
+            pl.semaphore_wait(word_sem.at[side], 1)
+
         pl.semaphore_signal(
-            barrier, inc=1, device_id={"comp": lax.rem(me + k, peers)}, device_id_type=MESH
+            word_sem.at[side], inc=1, device_id={"comp": me + step}, device_id_type=MESH
         )
-        count += 1
-    for k in (1, spaces - 1):
-        pl.semaphore_signal(
-            barrier, inc=1, device_id={"space": lax.rem(here + k, spaces)}, device_id_type=MESH
-        )
-        count += 1
-    return barrier, count
+
+    def up():
+        onward(0, me > 1, 1)
+
+    def down():
+        onward(1, me < peers - 2, -1)
+
+    inside = jnp.logical_and(me > 0, me < peers - 1)
+
+    @pl.when(jnp.logical_and(inside, me < peers // 2))
+    def _():
+        up()
+        down()
+
+    @pl.when(jnp.logical_and(inside, me >= peers // 2))
+    def _():
+        down()
+        up()
+
+
+def hear_word(peers, word_sem):
+    me = lax.axis_index("comp")
+    if peers > 2:
+        for side, last in ((1, me == 0), (0, me == peers - 1)):
+
+            @pl.when(last)
+            def _(side=side):
+                pl.semaphore_wait(word_sem.at[side], 1)
+
+
+def send_orders(peers):
+    orders = []
+    for me in range(peers):
+        low = me < peers // 2
+        others = [t for t in range(peers) if t != me]
+        across = sorted((t for t in others if (t < peers // 2) != low), key=lambda t: -abs(t - me))
+        beside = sorted((t for t in others if (t < peers // 2) == low), key=lambda t: abs(t - me))
+        inner = me in (peers // 2 - 1, peers // 2)
+        row = across + beside if inner else beside + across
+        orders.append([(t - me) % peers for t in row])
+    return orders
 
 
 def wave_kernel(
@@ -56,8 +111,19 @@
     block,
     batch,
     early,
-    late,
+    late_first,
+    late_second,
     field_ref,
+    wave_in,
+    substeps_in,
+    trig_in,
+    east_in,
+    north_in,
+    neighbour_in,
+    quad_in,
+    strength_in,
+    blocks_ref,
+    out_ref,
     wave_ref,
     substeps_ref,
     trig_ref,
@@ -66,8 +132,7 @@
     neighbour_ref,
     quad_ref,
     strength_ref,
-    blocks_ref,
-    out_ref,
+    small_sem,
     points_ref,
     extended,
     finals,
@@ -87,6 +152,7 @@
     products,
     slots,
     updated,
+    word_sem,
     load_sem,
     blocks_sem,
     chain_sem,
@@ -112,12 +178,28 @@
     odd = lax.rem(here, 2)
     goes_first = odd == jnp.where(here < spaces // 2, 0, 1)
 
+    barrier, greetings = greet(peers, spaces)
+    pairs = (
+        (neighbour_in, neighbour_ref),
+        (east_in, east_ref),
+        (north_in, north_ref),
+        (trig_in, trig_ref),
+        (substeps_in, substeps_ref),
+        (wave_in, wave_ref),
+        (quad_in, quad_ref),
+        (strength_in, strength_ref),
+    )
+    loads = [
+        pltpu.make_async_copy(source, target, small_sem.at[i])
+        for i, (source, target) in enumerate(pairs)
+    ]
+    for copy in loads:
+        copy.start()
     load = pltpu.make_async_copy(field_ref, extended.at[:, pl.ds(reach, width)], load_sem)
     load.start()
     load_blocks = pltpu.make_async_copy(blocks_ref, blocks, blocks_sem)
     load_blocks.start()
 
-    barrier, greetings = greet(peers, spaces)
     lane = lax.broadcasted_iota(jnp.int32, (4, HALO), 1)
     for side, missing in ((0, jnp.logical_not(has_left)), (1, jnp.logical_not(has_right))):
 
@@ -155,29 +237,9 @@
         fill(j + SUB, neighbour_ref, east_ref, north_ref, j, pl.ds(pl.multiple_of(j * HALO, HALO), HALO))
         return carry
 
+    for copy in loads[:3]:
+        copy.wait()
     lax.fori_loop(0, tiles, fill_own, 0)
-
-    total = blocks.shape[0]
-    spots = lax.broadcasted_iota(jnp.int32, (1, HALO), 1)
-    none = jnp.full((1, HALO), total, jnp.int32)
-
-    def targets(j, row):
-        return jnp.where(spots == j, quad_ref[3, j], row)
-
-    def link(j, carry):
-        before, last = carry
-        target = quad_ref[3, j]
-        before = jnp.where(jnp.logical_and(spots > j, row == target), j, before)
-        last = jnp.where(spots == target, j, last)
-        return before, last
-
-    row = lax.fori_loop(0, total, targets, none)
-    before, last = lax.fori_loop(0, total, link, (none, none))
-    links[0:1] = before
-    links[1:2] = last
-    load_chain = pltpu.make_async_copy(links, chain, chain_sem)
-    load_chain.start()
-    slots[total] = jnp.zeros((ND, HALO), jnp.float32)
 
     pl.semaphore_wait(barrier, greetings)
 
@@ -199,9 +261,9 @@
         for side, start, device in ((1, 0, left), (0, width - reach, right)):
             part = pl.ds(start, reach)
             pairs = (
-                (neighbour_ref.at[:, part], side_table.at[side]),
-                (east_ref.at[:, part], side_current.at[side, 0]),
-                (north_ref.at[:, part], side_current.at[side, 1]),
+                (neighbour_in.at[:, part], side_table.at[side]),
+                (east_in.at[:, part], side_current.at[side, 0]),
+                (north_in.at[:, part], side_current.at[side, 1]),
             )
             copies.append(
                 [
@@ -258,6 +320,7 @@
         return carry
 
     lax.fori_loop(0, chunks, start_halo, 0)
+    pass_word(peers, word_sem)
 
     @pl.when(has_right)
     def _():
@@ -269,9 +332,11 @@
         for copy in to_right_sides:
             copy.wait_recv()
 
-    for i in range(SUB):
+    for i in range(1, SUB):
         place = pl.ds(i * HALO, HALO)
         fill(i, side_table.at[0], side_current.at[0, 0], side_current.at[0, 1], tiles - SUB + i, place)
+    for i in range(SUB - 1):
+        place = pl.ds(i * HALO, HALO)
         fill(
             SUB + tiles + i, side_table.at[1], side_current.at[1, 0], side_current.at[1, 1], i, place
         )
@@ -365,8 +430,19 @@
             {"comp": target},
         )
 
-    order = sorted(range(1, peers), key=lambda k: abs(k - peers / 2))
+    orders = send_orders(peers)
+    order = []
+    for place in range(peers - 1):
+        k = orders[0][place]
+        for other in range(1, peers):
+            k = jnp.where(me == other, orders[other][place], k)
+        order.append(k)
+    steps = range(1, peers)
+    for copy in loads[3:]:
+        copy.wait()
     load.wait()
+
+    late = jnp.where(goes_first, late_first, late_second)
 
     def step(c, carry):
         first = rows_of(c)
@@ -389,6 +465,10 @@
         else:
             lax.fori_loop(0, tiles // block, per_block, 0)
 
+        @pl.when(c == 0)
+        def _():
+            hear_word(peers, word_sem)
+
         @pl.when(jnp.logical_or(goes_first, c < early))
         def _():
             for k in order:
@@ -400,34 +480,55 @@
     place = pl.ds(pl.multiple_of(me * rows, 8), rows)
     own = pltpu.make_async_copy(finals.at[me], points_ref.at[place], own_sem)
     own.start()
-    most = (chunks - late) * chunk
+    most_first = (chunks - late_first) * chunk
+    most_second = (chunks - late_second) * chunk
+    partner = {"space": here + 1 - 2 * odd}
+
+    @pl.when(goes_first)
+    def _():
+        for k in steps:
+            piece(k, 0, most_first, 0).wait_send()
+        pl.semaphore_signal(turn_sem.at[0], inc=1, device_id=partner, device_id_type=MESH)
 
     @pl.when(jnp.logical_not(goes_first))
     def _():
         pl.semaphore_wait(turn_sem.at[0], 1)
-        if early < chunks - late:
+        if early * chunk < most_second:
             for k in order:
-                piece(k, early * chunk, most - early * chunk, 0).start()
-        if late:
+                piece(k, early * chunk, most_second - early * chunk, 0).start()
+        if late_second:
             for k in order:
-                piece(k, most, rows - most, 1).start()
-
-    for k in order:
-        piece(k, 0, most, 0).wait_send()
-    partner = {"space": here + 1 - 2 * odd}
-
-    @pl.when(goes_first)
-    def _():
-        pl.semaphore_signal(turn_sem.at[0], inc=1, device_id=partner, device_id_type=MESH)
-
-    @pl.when(jnp.logical_not(goes_first))
-    def _():
+                piece(k, most_second, rows - most_second, 1).start()
+        for k in steps:
+            piece(k, 0, most_second, 0).wait_send()
         pl.semaphore_signal(turn_sem.at[1], inc=1, device_id=partner, device_id_type=MESH)
+
+    total = blocks.shape[0]
+    spots = lax.broadcasted_iota(jnp.int32, (1, HALO), 1)
+    none = jnp.full((1, HALO), total, jnp.int32)
+
+    def targets(j, row):
+        return jnp.where(spots == j, quad_ref[3, j], row)
+
+    def link(j, carry):
+        before, last = carry
+        target = quad_ref[3, j]
+        before = jnp.where(jnp.logical_and(spots > j, row == target), j, before)
+        last = jnp.where(spots == target, j, last)
+        return before, last
+
+    row = lax.fori_loop(0, total, targets, none)
+    before, last = lax.fori_loop(0, total, link, (none, none))
+    links[0:1] = before
+    links[1:2] = last
+    load_chain = pltpu.make_async_copy(links, chain, chain_sem)
+    load_chain.start()
+    slots[total] = jnp.zeros((ND, HALO), jnp.float32)
 
     own.wait()
     load_blocks.wait()
     load_chain.wait()
-    for k in order:
+    for k in steps:
         piece(k, 0, rows, 0).wait_recv()
 
     def frequency(f):
@@ -505,9 +606,14 @@
             copy.wait_send()
 
     own.wait()
-    if late:
-        for k in order:
-            piece(k, most, rows - most, 1).wait_send()
+    for turn, most in ((goes_first, most_first), (jnp.logical_not(goes_first), most_second)):
+        if most < rows:
+
+            @pl.when(turn)
+            def _(most=most):
+                for k in steps:
+                    piece(k, most, rows - most, 1).wait_send()
+
     for home in homes:
         home.wait()
 
@@ -525,20 +631,29 @@
     outer = tiles + 2 * SUB
     window = block + 2 * SUB
     batch = math.gcd(total, 32)
-    late = min(LATE, rows // chunk - 1)
-    early = min(EARLY, rows // chunk - late)
+    late_first = min(LATE_FIRST, rows // chunk - 1)
+    late_second = min(LATE_SECOND, rows // chunk - 1)
+    early = min(EARLY, rows // chunk - late_second)
     angles = (np.arange(ND, dtype=np.float32) + np.float32(0.5)) * np.float32(2.0 * math.pi / ND)
     trig = np.stack([np.cos(angles), np.sin(angles)])
     trig = np.ascontiguousarray(np.broadcast_to(trig[:, :, None], (2, ND, HALO)))
     vmem = pl.BlockSpec(memory_space=pltpu.VMEM)
-    smem = pl.BlockSpec(memory_space=pltpu.SMEM)
     whole = pl.BlockSpec(memory_space=pl.ANY)
     return pl.pallas_call(
-        functools.partial(wave_kernel, peers, spaces, chunk, block, batch, early, late),
+        functools.partial(wave_kernel, peers, spaces, chunk, block, batch, early, late_first, late_second),
         out_shape=pltpu.VMEM((rows, width), jnp.float32),
-        in_specs=[whole, smem, smem, vmem, vmem, vmem, vmem, smem, smem, whole],
+        in_specs=[whole] * 10,
         out_specs=vmem,
         scratch_shapes=[
+            pltpu.SMEM(wave_speed.shape, jnp.float32),
+            pltpu.SMEM(substeps.shape, jnp.int32),
+            pltpu.VMEM((2, ND, HALO), jnp.float32),
+            pltpu.VMEM((1, width), jnp.float32),
+            pltpu.VMEM((1, width), jnp.float32),
+            pltpu.VMEM((4, width), jnp.int32),
+            pltpu.SMEM(quad_index.shape, jnp.int32),
+            pltpu.SMEM(strength.shape, jnp.float32),
+            pltpu.SemaphoreType.DMA((8,)),
             pltpu.VMEM((peers * rows, HALO), jnp.float32),
             pltpu.VMEM((rows, width + 2 * reach), jnp.float32),
             pltpu.VMEM((tiles, rows, HALO), jnp.float32),
@@ -558,6 +673,7 @@
             pltpu.VMEM((batch, ND, HALO), jnp.bfloat16),
             pltpu.VMEM((total + 1, ND, HALO), jnp.float32),
             pltpu.VMEM((peers * rows, HALO), jnp.float32),
+            pltpu.SemaphoreType.REGULAR((2,)),
             pltpu.SemaphoreType.DMA,
             pltpu.SemaphoreType.DMA,
             pltpu.SemaphoreType.DMA,

time: 61.1 us -> 60.5 us (level)
    pallas_call x1, Pallas kernels: 59.9 us -> 59.3 us  [advance_waves(): pl.pallas_call(functools.partial(wave_kernel, peers, spaces, chunk, block...]
where the time goes in v4:
time: 60.5 us; the launch traced here: 60.3 us
  Pallas kernels  59.3 us (98%)
  local copies, waits for them, and re-layouts  1.02 us (2%)
    pallas_call x1, Pallas kernels, advance_waves(): pl.pallas_call(functools.partial(wave_kernel, peers, spaces, chunk, block...  59.3 us

profile of v4, /device:TPU:9, one launch (start us, length us, event | category | flops | bytes accessed | tf_op | source)
XLA Modules:
  0.0 60.3 jit_solution(3101093105655079584)
XLA Ops:
  0.0 59.3 %shard_map.100 = f32[576,512]{1,0:T(8,128)S(1)} custom-call(f32[576,512]{1,0:T(8,128)} %field_ref.1, f32[36]{0:T(128)} %wave_in.1, s32[2304]{0:T(1024)} %substeps_in.1, f32[2,64,128]{2,1,0:T(8,128)} %constant.2.clone.trig_in, f32[1,512]{1,0:T(1,128)} %bitcast.2, f32[1,512]{1,0:T(1,128)} %bitcast.3, s32[4,512]{1,0:T(4,128)} %neighbour_in.1, s32[4,64]{1,0:T(4,128)} %quad_in.1, ...), custom_call_target="tpu_custom_call" | custom-call | tf_op jit(solution)/shard_map/pallas_call | solution.py:642
  59.3 1.0 %copy.12 = f32[576,512]{1,0:T(8,128)} copy(f32[576,512]{1,0:T(8,128)S(1)} %shard_map.100) | data formatting | bytes 2359296

commit v5 on v4

--- a/solution.py
+++ b/solution.py
@@ -332,19 +332,26 @@
         for copy in to_right_sides:
             copy.wait_recv()
 
-    for i in range(1, SUB):
-        place = pl.ds(i * HALO, HALO)
-        fill(i, side_table.at[0], side_current.at[0, 0], side_current.at[0, 1], tiles - SUB + i, place)
-    for i in range(SUB - 1):
-        place = pl.ds(i * HALO, HALO)
-        fill(
-            SUB + tiles + i, side_table.at[1], side_current.at[1, 0], side_current.at[1, 1], i, place
-        )
+    trimmed = tiles == block
+
+    @pl.when(jnp.logical_or(has_left, not trimmed))
+    def _():
+        for i in range(1, SUB):
+            place = pl.ds(i * HALO, HALO)
+            east_row, north_row = side_current.at[0, 0], side_current.at[0, 1]
+            fill(i, side_table.at[0], east_row, north_row, tiles - SUB + i, place)
+
+    @pl.when(jnp.logical_or(has_right, not trimmed))
+    def _():
+        for i in range(SUB - 1):
+            place = pl.ds(i * HALO, HALO)
+            east_row, north_row = side_current.at[1, 0], side_current.at[1, 1]
+            fill(SUB + tiles + i, side_table.at[1], east_row, north_row, i, place)
 
     sublane = lax.broadcasted_iota(jnp.int32, (8, HALO), 0)
     window = block + 2 * SUB
 
-    def prepare(first, base):
+    def prepare(first, base, low, high):
         def per_group(g, carry):
             at = pl.ds(pl.multiple_of(g * 8, 8), 8)
             component = me * rows + first + g * 8
@@ -358,7 +365,7 @@
             count = taken.astype(jnp.float32)
             repeats[at] = count
             scale = courant_scale / count
-            for i in range(1, window - 1):
+            for i in range(low, high):
                 along_x = (own_x + currents[0, base + i]) * scale
                 along_y = (own_y + currents[1, base + i]) * scale
                 speeds[0, i, at] = jnp.clip(along_x, -courant_limit, courant_limit)
@@ -385,10 +392,12 @@
                 taken = term if taken is None else taken + term
         return taken[:, :HALO], taken[:, HALO:]
 
-    def advance(first, b):
+    def advance(first, b, open_left=True, open_right=True):
         base = b * block
         at = pl.ds(first, chunk)
-        prepare(first, base)
+        low = 0 if open_left else SUB - 1
+        high = window if open_right else window - SUB + 1
+        prepare(first, base, low + 1, high - 1)
 
         def state(s, i):
             if s == 0:
@@ -396,14 +405,15 @@
             return states[s % 2, i]
 
         for s in range(SUB):
-            for i in range(s, window - s):
+            edge = min(s, 1)
+            for i in range(max(s, low + edge), min(window - s, high - edge)):
                 rest = state(s, i)
                 for p in range(PARTS):
                     part = rest.astype(jnp.bfloat16)
                     parts[i, p * chunk : (p + 1) * chunk] = part
                     if p + 1 < PARTS:
                         rest = rest - part.astype(jnp.float32)
-            for i in range(s + 1, window - 1 - s):
+            for i in range(max(s, low) + 1, min(window - s, high) - 1):
                 value = state(s, i)
                 west, south = pick(i - 1, selector[base + i, 0])
                 east, north = pick(i, selector[base + i, 1])
@@ -460,8 +470,20 @@
             advance(first, b)
             return inner
 
-        if tiles == block:
-            advance(first, 0)
+        if trimmed:
+
+            @pl.when(jnp.logical_and(has_left, has_right))
+            def _():
+                advance(first, 0)
+
+            @pl.when(jnp.logical_not(has_left))
+            def _():
+                advance(first, 0, open_left=False)
+
+            @pl.when(jnp.logical_not(has_right))
+            def _():
+                advance(first, 0, open_right=False)
+
         else:
             lax.fori_loop(0, tiles // block, per_block, 0)
 

time: 60.5 us -> 60.1 us (level)
  no operation moved by 1% of the time
where the time goes in v5:
time: 60.1 us; the launch traced here: 59.9 us
  Pallas kernels  58.8 us (98%)
  local copies, waits for them, and re-layouts  1.02 us (2%)
    pallas_call x1, Pallas kernels, advance_waves(): pl.pallas_call(functools.partial(wave_kernel, peers, spaces, chunk, block...  58.8 us

profile of v5, /device:TPU:9, one launch (start us, length us, event | category | flops | bytes accessed | tf_op | source)
XLA Modules:
  0.0 59.9 jit_solution(9156452342456700137)
XLA Ops:
  0.0 58.8 %shard_map.100 = f32[576,512]{1,0:T(8,128)S(1)} custom-call(f32[576,512]{1,0:T(8,128)} %field_ref.1, f32[36]{0:T(128)} %wave_in.1, s32[2304]{0:T(1024)} %substeps_in.1, f32[2,64,128]{2,1,0:T(8,128)} %constant.2.clone.trig_in, f32[1,512]{1,0:T(1,128)} %bitcast.2, f32[1,512]{1,0:T(1,128)} %bitcast.3, s32[4,512]{1,0:T(4,128)} %neighbour_in.1, s32[4,64]{1,0:T(4,128)} %quad_in.1, ...), custom_call_target="tpu_custom_call" | custom-call | tf_op jit(solution)/shard_map/pallas_call | solution.py:664
  58.8 1.0 %copy.12 = f32[576,512]{1,0:T(8,128)} copy(f32[576,512]{1,0:T(8,128)S(1)} %shard_map.100) | data formatting | bytes 2359296

commit v6 on v5

--- a/solution.py
+++ b/solution.py
@@ -725,6 +725,23 @@
     )
 
 
+def store_kernel(new_ref, out_ref, sem):
+    copy = pltpu.make_async_copy(new_ref, out_ref, sem)
+    copy.start()
+    copy.wait()
+
+
+def store(new):
+    return pl.pallas_call(
+        store_kernel,
+        out_shape=jax.ShapeDtypeStruct(new.shape, new.dtype),
+        in_specs=[pl.BlockSpec(memory_space=pltpu.VMEM)],
+        out_specs=pl.BlockSpec(memory_space=pl.ANY),
+        scratch_shapes=[pltpu.SemaphoreType.DMA],
+        compiler_params=pltpu.CompilerParams(vmem_limit_bytes=1 << 20),
+    )(new)
+
+
 def shards(
     spectrum,
     wave_speed,
@@ -740,7 +757,7 @@
     spaces = lax.axis_size("space")
     rows, width = spectrum.shape
     assert width == peers * HALO
-    return advance_waves(
+    new = advance_waves(
         spectrum,
         wave_speed,
         substeps,
@@ -753,6 +770,7 @@
         peers,
         spaces,
     )
+    return store(new)
 
 
 def solution(mesh):

time: 60.1 us -> 60.1 us (level)
  Pallas kernels: 58.8 us -> 59.9 us
  local copies, waits for them, and re-layouts: 1.02 us -> 0 us
    pallas_call x0 -> x1, Pallas kernels: none -> 1.02 us  [store(): pl.pallas_call(store_kernel, out_shape=jax.ShapeDtypeStruct(new.shape, ne...]
    unnamed x1 -> x0, local copies, waits for them, and re-layouts: 1.02 us -> none
where the time goes in v6:
time: 60.1 us; the launch traced here: 59.9 us
  Pallas kernels  59.9 us (100%)
    pallas_call x1, Pallas kernels, advance_waves(): pl.pallas_call(functools.partial(wave_kernel, peers, spaces, chunk, block...  58.8 us

profile of v6, /device:TPU:9, one launch (start us, length us, event | category | flops | bytes accessed | tf_op | source)
XLA Modules:
  0.0 59.9 jit_solution(8985179799340184168)
XLA Ops:
  0.0 58.8 %shard_map.100.new_ref = f32[576,512]{1,0:T(8,128)S(1)} custom-call(f32[576,512]{1,0:T(8,128)} %field_ref.1, f32[36]{0:T(128)} %wave_in.1, s32[2304]{0:T(1024)} %substeps_in.1, f32[2,64,128]{2,1,0:T(8,128)} %constant.2.clone.trig_in, f32[1,512]{1,0:T(1,128)} %bitcast.2, f32[1,512]{1,0:T(1,128)} %bitcast.3, s32[4,512]{1,0:T(4,128)} %neighbour_in.1, ...), custom_call_target="tpu_custom_call" | custom-call | tf_op jit(solution)/shard_map/pallas_call | solution.py:664
  58.8 1.0 %shard_map.101 = f32[576,512]{1,0:T(8,128)} custom-call(f32[576,512]{1,0:T(8,128)S(1)} %shard_map.100.new_ref), custom_call_target="tpu_custom_call" | custom-call | tf_op jit(solution)/shard_map/pallas_call | solution.py:735

commit v7 on v6

--- a/solution.py
+++ b/solution.py
@@ -210,14 +210,15 @@
                 part = pl.ds(i * HALO, HALO)
                 side_table[side, :, part] = lane + (first + (i + 1) * HALO)
             side_current[side] = jnp.zeros((2, 1, reach), jnp.float32)
-            start = 0 if side == 0 else reach + width
+            depth = HALO if tiles == block else reach
+            start = reach - depth if side == 0 else reach + width
 
             def clear(g, carry):
                 at = pl.ds(pl.multiple_of(g * 8, 8), 8)
-                extended[at, pl.ds(start, reach)] = jnp.zeros((8, reach), jnp.float32)
+                extended[at, pl.ds(start, depth)] = jnp.zeros((8, depth), jnp.float32)
                 return carry
 
-            lax.fori_loop(0, rows // 8, clear, 0)
+            lax.fori_loop(0, rows // 8, clear, 0, unroll=8 if rows % 64 == 0 else 1)
 
     def spread(row):
         return jnp.broadcast_to(row, (8, HALO))

time: 60.1 us -> 60.1 us (level)
  no operation moved by 1% of the time
where the time goes in v7:
time: 60.1 us; the launch traced here: 59.9 us
  Pallas kernels  59.9 us (100%)
    pallas_call x1, Pallas kernels, advance_waves(): pl.pallas_call(functools.partial(wave_kernel, peers, spaces, chunk, block...  58.8 us

profile of v7, /device:TPU:9, one launch (start us, length us, event | category | flops | bytes accessed | tf_op | source)
XLA Modules:
  0.0 59.9 jit_solution(4617079988761992776)
XLA Ops:
  0.0 58.8 %shard_map.100.new_ref = f32[576,512]{1,0:T(8,128)S(1)} custom-call(f32[576,512]{1,0:T(8,128)} %field_ref.1, f32[36]{0:T(128)} %wave_in.1, s32[2304]{0:T(1024)} %substeps_in.1, f32[2,64,128]{2,1,0:T(8,128)} %constant.2.clone.trig_in, f32[1,512]{1,0:T(1,128)} %bitcast.2, f32[1,512]{1,0:T(1,128)} %bitcast.3, s32[4,512]{1,0:T(4,128)} %neighbour_in.1, ...), custom_call_target="tpu_custom_call" | custom-call | tf_op jit(solution)/shard_map/pallas_call | solution.py:665
  58.8 1.0 %shard_map.101 = f32[576,512]{1,0:T(8,128)} custom-call(f32[576,512]{1,0:T(8,128)S(1)} %shard_map.100.new_ref), custom_call_target="tpu_custom_call" | custom-call | tf_op jit(solution)/shard_map/pallas_call | solution.py:736
